TPU v7x, 256 devices: a whole 4x4x8 slice. The times are simulated.
256 devices in a mesh: space: 32 (over y_hi, z, core), coil: 8 (over y_lo, x).
Axes of the slice: x: 4, y: 4 (y_hi: 2, y_lo: 2; y = y_hi * 2 + y_lo), z: 8, core: 2. Of those that a mesh axis runs over, the one named last changes fastest.
Arguments:
- spatial_coef: bfloat16 [16, 128, 128, 2, 128], P('coil', 'space'), may hold values from -6 to 6
- temporal_basis: bfloat16 [2, 16, 4], replicated, may hold values from -1.5 to 1.5
- coil_maps: bfloat16 [32, 128, 128, 2, 128], P('coil', 'space'), may hold values from -6 to 6
- field_steps: int32 [128, 128, 128], P('space'), may hold values from 0 to 255
- kspace_data: bfloat16 [32, 4, 128, 128, 2, 128], P('coil', None, None, 'space'), may hold values from -6 to 6
- sample_mask: int32 [4, 128, 128], P(None, 'space'), may hold values 0 or 1
Outputs:
- gradient: float32 [16, 128, 128, 2, 128], P('coil', 'space')
Inputs may be any that keep to these rules, and one draw needn't show every extreme that they name: `sample_mask`: 1 where a phase-encoding line is sampled at that point, else 0.
All inputs are finite; a program needn't handle non-finite values. No bound on the sum of `sample_mask` on one device may be relied on, other than what follows from the above.
Results may differ from a plain program's by a relative error of at most 0.014.
Values may be sent and summed in bfloat16 or wider, within the bound.
A program may use at most 64 MiB of HBM per device.

v0:
```python
import math
import jax
import jax.numpy as jnp
from jax import lax
from jax.sharding import PartitionSpec as P

STEPS_CYCLE = 256


def dft_table(length, sign):
    index = jnp.arange(length, dtype=jnp.int32)
    steps = index[:, None] * index[None, :] % length
    angle = steps.astype(jnp.float32) * (2.0 * math.pi / length)
    scale = 1.0 / math.sqrt(length)
    cosine = jnp.cos(angle) * scale
    sine = jnp.sin(angle) * (sign * scale)
    upper = jnp.stack([cosine, sine], axis=1)
    lower = jnp.stack([-sine, cosine], axis=1)
    return jnp.stack([upper, lower], axis=0).astype(jnp.bfloat16)


def forward_mix(basis):
    real_part = basis[0]
    imaginary = basis[1]
    return jnp.stack(
        [jnp.stack([real_part, imaginary], -1), jnp.stack([-imaginary, real_part], -1)], 1
    )


def adjoint_mix(basis):
    real_part = basis[0].T
    imaginary = basis[1].T
    return jnp.stack(
        [jnp.stack([real_part, -imaginary], -1), jnp.stack([imaginary, real_part], -1)], 1
    )


def phase_parts(field_steps, points):
    counter = jnp.arange(1, points + 1, dtype=jnp.int32)
    steps = field_steps[None] * counter[:, None, None, None] % STEPS_CYCLE
    angle = steps.astype(jnp.float32) * (2.0 * math.pi / STEPS_CYCLE)
    return (jnp.cos(angle), jnp.sin(angle))


def transform(volume, table, form):
    return jnp.einsum(form, volume, table, preferred_element_type=jnp.float32)


def shards(spatial_coef, temporal_basis, coil_maps, field_steps, kspace_data, sample_mask):
    points = temporal_basis.shape[2]
    section = temporal_basis
    data_first = transform(
        kspace_data, dft_table(kspace_data.shape[2], 1.0), "ctxypz,pxqk->ctkyqz"
    ).astype(jnp.bfloat16)
    measured = lax.all_to_all(data_first, "space", split_axis=2, concat_axis=3, tiled=True)
    mask_all = lax.all_gather(sample_mask.astype(jnp.bfloat16), "space", axis=1, tiled=True)
    mask_all = mask_all.astype(jnp.float32)[None, :, None, :, None, :]
    image = jnp.einsum(
        "lxypz,lptq->txyqz",
        lax.all_gather(spatial_coef, "coil", axis=0, tiled=True),
        forward_mix(section),
        preferred_element_type=jnp.float32,
    )
    cosine, sine = phase_parts(field_steps, points)
    image_real = image[:, :, :, 0]
    image_imaginary = image[:, :, :, 1]
    turned_real = cosine * image_real - sine * image_imaginary
    turned_imaginary = sine * image_real + cosine * image_imaginary
    map_real = coil_maps[:, :, :, 0].astype(jnp.float32)[:, None]
    map_imaginary = coil_maps[:, :, :, 1].astype(jnp.float32)[:, None]
    coil_real = map_real * turned_real - map_imaginary * turned_imaginary
    coil_imaginary = map_real * turned_imaginary + map_imaginary * turned_real
    coil_image = jnp.stack([coil_real, coil_imaginary], axis=4).astype(jnp.bfloat16)
    depth_count = coil_image.shape[5]
    row_count = coil_image.shape[3]
    depth_pass = transform(coil_image, dft_table(depth_count, -1.0), "ctxypz,pzqk->ctxyqk").astype(
        jnp.bfloat16
    )
    row_pass = transform(depth_pass, dft_table(row_count, -1.0), "ctxypz,pyqk->ctxkqz")
    residual = (mask_all * (row_pass - measured.astype(jnp.float32))).astype(jnp.bfloat16)
    back_rows = transform(residual, dft_table(row_count, 1.0), "ctxypz,pyqk->ctxkqz").astype(
        jnp.bfloat16
    )
    back_image = transform(back_rows, dft_table(depth_count, 1.0), "ctxypz,pzqk->ctxyqk")
    back_real = back_image[:, :, :, :, 0]
    back_imaginary = back_image[:, :, :, :, 1]
    sum_real = jnp.sum(map_real * back_real + map_imaginary * back_imaginary, axis=0)
    sum_imaginary = jnp.sum(map_real * back_imaginary - map_imaginary * back_real, axis=0)
    combined_real = cosine * sum_real + sine * sum_imaginary
    combined_imaginary = cosine * sum_imaginary - sine * sum_real
    combined = jnp.stack([combined_real, combined_imaginary], axis=3)
    section = temporal_basis.astype(jnp.float32)
    return lax.psum_scatter(
        jnp.einsum(
            "txypz,tplq->lxyqz", combined, adjoint_mix(section), precision=lax.Precision.HIGHEST
        ).astype(jnp.bfloat16),
        "coil",
        scatter_dimension=0,
        tiled=True,
    ).astype(jnp.float32)


def solution(mesh):
    in_specs = (
        P("coil", "space", None, None, None),
        P(),
        P("coil", "space", None, None, None),
        P("space", None, None),
        P("coil", None, None, "space", None, None),
        P(None, "space", None),
    )
    out_specs = P("coil", "space", None, None, None)
    return jax.shard_map(shards, mesh=mesh, in_specs=in_specs, out_specs=out_specs, check_vma=False)
```

profile of v0, /device:TPU:1, one launch (start us, length us, event | category | flops | bytes accessed | tf_op | source)
XLA Modules:
  0.0 291.8 jit_solution(16822251822179773445)
XLA Ops:
  6.5 1.9 copy.62
  8.5 0.0 all-gather.2.cloned.1.call-update
  8.5 0.3 negate_convert_fusion
  8.8 0.3 multiply_convert_fusion
  9.1 0.3 multiply_convert_fusion.2
  9.3 0.7 fusion.59
  10.0 3.5 %fusion.5 = bf16[4,4,128,4,2,128]{5,2,3,1,0,4:T(8,128)(2,1)S(1)} fusion(bf16[4,4,128,4,2,128]{5,4,3,2,1,0:T(2,128)(2,1)} %param.10, bf16[1,128,2,128]{3,1,2,0:T(8,128)(2,1)S(1)} %get-tuple-element.17, bf16[1,128,2,128]{3,1,2,0:T(8,128)(2,1)S(1)} %get-tuple-element.18), kind=kOutput, calls=%fused_computation.9 | convolution fusion | flops 1075904512 | bytes 8519680 | tf_op jit(solution)/shard_map/ctxypz,pxqk->ctkyqz/dot_general | solution.py:46
  13.5 5.2 %copy.68 = bf16[4,4,128,4,2,128]{5,3,1,0,4,2:T(4,128)(2,1)} copy(bf16[4,4,128,4,2,128]{5,2,3,1,0,4:T(8,128)(2,1)S(1)} %fusion.5) | data formatting | bytes 8388608 | tf_op jit(solution)/shard_map/convert_element_type | solution.py:54
  18.7 12.9 %all-to-all-start = ((bf16[4,4,128,4,2,128]{5,3,1,0,4,2:T(4,128)(2,1)}), bf16[4,4,128,4,2,128]{5,3,1,0,4,2:T(4,128)(2,1)}, u32[]{:S(2)}, u32[]{:S(2)}) async-start(bf16[4,4,128,4,2,128]{5,3,1,0,4,2:T(4,128)(2,1)} %copy.68), calls=%async_computation | async-start | bytes 8388608 | tf_op jit(solution)/shard_map/all_to_all | solution.py:55
  31.7 0.0 reduce-scatter.2.cloned.1.call-start
  31.7 0.0 copy-done.4
  31.8 0.0 copy-done.5
  31.8 135.0 %all_gather.6 = bf16[4,128,128]{2,0,1:T(4,128)(2,1)S(1)} all-gather(bf16[4,4,128]{2,0,1:T(4,128)(2,1)S(1)} %copy_convert_fusion.1), channel_id=1, replica_groups=mesh['space'=32,'coil'=8] {'space'}, dimensions={1}, use_global_device_ids=true | all-gather | bytes 135168 | tf_op jit(solution)/shard_map/all_gather | solution.py:56
  166.8 0.5 iota_add_fusion
  167.4 2.2 slice_convert_fusion.1
  169.6 0.0 all-gather.2.cloned.1.call-done
  169.6 0.0 copy-start.1
  169.7 4.9 %fusion.36 = f32[4,2,4,128,128]{4,0,3,2,1:T(4,128)S(1)} fusion(bf16[16,4,128,2,128]{4,2,3,1,0:T(8,128)(2,1)} %all-gather.2.cloned.1.call-done, bf16[16,1,4,2]{0,2,1,3:T(4,128)(2,1)S(1)} %get-tuple-element.26, bf16[16,1,4,2]{0,2,1,3:T(4,128)(2,1)S(1)} %get-tuple-element.25), kind=kOutput, calls=%fused_computation.43 | convolution fusion | flops 33555456 | bytes 6291968 | tf_op jit(solution)/shard_map/lxypz,lptq->txyqz/dot_general | solution.py:58
  174.5 0.3 copy.124
  174.8 4.6 %multiply_subtract_fusion = (f32[4,4,128,128]{3,2,1,0:T(8,128)S(1)}, f32[4,4,128,128]{3,2,1,0:T(8,128)S(1)}) fusion(f32[4,4,128,2,128]{4,2,1,0,3:T(8,128)S(1)} %bitcast.236, s32[4]{0:T(128)S(1)} %copy-done.6, s32[4,128,128]{2,1,0:T(8,128)S(1)} %copy-done.1), kind=kLoop, calls=%fused_computation.64 | loop fusion | flops 5242880 | bytes 4456464 | tf_op jit(solution)/shard_map/sub | solution.py:67
  179.5 3.1 %subtract_convert_fusion = (bf16[4,4,4,128,1,128]{5,3,4,2,1,0:T(8,128)(2,1)}, bf16[4,4,4,128,1,128]{5,3,4,2,1,0:T(8,128)(2,1)}) fusion(f32[4,4,128,128]{3,2,1,0:T(8,128)S(1)} %get-tuple-element.12, f32[4,4,128,128]{3,2,1,0:T(8,128)S(1)} %bitcast.234, f32[4,4,128,128]{3,2,1,0:T(8,128)S(1)} %get-tuple-element.11, f32[4,4,128,128]{3,2,1,0:T(8,128)S(1)} %bitcast.232), kind=kLoop, calls=%fused_computation.30 | loop fusion | flops 8388608 | bytes 8388608 | tf_op jit(solution)/shard_map/convert.5
  182.5 8.0 %fusion.3 = f32[2,128,4,4,4,128,1]{5,1,6,0,4,3,2:T(8,128)} fusion(bf16[4,4,4,128,1,128]{5,3,4,2,1,0:T(8,128)(2,1)} %get-tuple-element.8, bf16[4,4,4,128,1,128]{5,3,4,2,1,0:T(8,128)(2,1)} %get-tuple-element.7, bf16[1,128,2,128]{3,1,0,2:T(8,128)(2,1)S(1)} %copy-done.3, bf16[1,128,2,128]{3,1,0,2:T(8,128)(2,1)S(1)} %copy-done.2), kind=kOutput, calls=%fused_computation.8 | convolution fusion | flops 2158493696 | bytes 12713984 | tf_op jit(solution)/shard_map/ctxypz,pyqk->ctxkqz/dot_general | solution.py:46
  190.5 0.0 all-to-all-done
  190.5 7.6 %copy.69 = f32[4,4,32,4,4,2,128]{6,4,2,5,3,1,0:T(4,128)} copy(bf16[4,4,32,4,4,2,128]{6,4,1,0,5,3,2:T(4,128)(2,1)} %bitcast.88) | data formatting | bytes 12582912 | tf_op jit(solution)/shard_map/convert_element_type | solution.py:80
  198.1 11.5 %fusion.27 = f32[4,4,4,128,2,128]{5,3,4,2,1,0:T(8,128)} fusion(f32[4,4,4,128,2,128]{5,3,4,2,1,0:T(8,128)} %bitcast.231, f32[2,128,4,4,4,128,1]{5,1,6,0,4,3,2:T(8,128)} %fusion.3, f32[4,128,128]{2,1,0:T(8,128)S(1)} %copy_convert_fusion, bf16[1,128,2,128]{3,1,2,0:T(8,128)(2,1)S(1)} %get-tuple-element.17, bf16[1,128,2,128]{3,1,2,0:T(8,128)(2,1)S(1)} %get-tuple-element.18), kind=kOutput, calls=%fused_computation.32 | convolution fusion | flops 2156396544 | bytes 25559040 | tf_op jit(solution)/shard_map/ctxypz,pzqk->ctxyqk/dot_general | solution.py:46
  209.6 4.3 %add_reduce_fusion = (f32[4,4,128,128]{3,2,1,0:T(8,128)S(1)}, f32[4,4,128,128]{3,2,1,0:T(8,128)S(1)}) fusion(f32[4,4,4,128,2,128]{5,3,4,2,1,0:T(8,128)} %fusion.27, f32[4,4,128,128]{3,2,1,0:T(8,128)S(1)} %bitcast.235, f32[4,4,128,128]{3,2,1,0:T(8,128)S(1)} %bitcast.233), kind=kLoop, calls=%fused_computation.28 | loop fusion | flops 7864320 | bytes 12582912 | tf_op jit(solution)/shard_map/reduce_sum | solution.py:87
  213.9 9.6 %fusion.45 = (f32[4,4,128,1,128]{4,0,3,2,1:T(4,128)S(1)}, f32[4,4,128,1,128]{4,0,3,2,1:T(4,128)S(1)}) fusion(f32[4,4,128,128]{3,2,1,0:T(8,128)S(1)} %get-tuple-element.6, f32[4,4,128,128]{3,2,1,0:T(8,128)S(1)} %get-tuple-element.5, s32[4]{0:T(128)S(1)} %copy-done.6, s32[4,128,128]{2,1,0:T(8,128)S(1)} %copy-done.1), kind=kLoop, calls=%fused_computation.58 | loop fusion | flops 5242880 | bytes 4456464 | tf_op jit(solution)/shard_map/add | solution.py:89
  223.6 8.0 %fusion.6 = bf16[16,4,128,2,128]{4,0,2,1,3:T(8,128)(2,1)S(1)} fusion(f32[4,4,128,1,128]{4,0,3,2,1:T(4,128)S(1)} %get-tuple-element.10, f32[4,4,128,1,128]{4,0,3,2,1:T(4,128)S(1)} %get-tuple-element.9, f32[4,1,16,2]{2,0,1,3:T(4,128)S(1)} %get-tuple-element.22, f32[4,1,16,2]{2,0,1,3:T(4,128)S(1)} %get-tuple-element.21), kind=kOutput, calls=%fused_computation.10 | convolution fusion | flops 203948288 | bytes 6292480 | tf_op jit(solution)/shard_map/txypz,tplq->lxyqz/dot_general | solution.py:94
  231.6 3.1 %copy.75 = bf16[16,4,128,2,128]{4,2,3,1,0:T(8,128)(2,1)} copy(bf16[16,4,128,2,128]{4,0,2,1,3:T(8,128)(2,1)S(1)} %fusion.6) | data formatting | bytes 8388608 | tf_op jit(solution)/shard_map/convert_element_type | solution.py:96
  234.6 0.0 reduce-scatter.2.cloned.1.call-update
  234.7 47.7 %reduce-scatter.2.cloned.1.call-done = bf16[2,4,128,2,128]{4,2,3,1,0:T(8,128)(2,1)} async-done(((bf16[16,4,128,2,128]{4,2,3,1,0:T(8,128)(2,1)}), bf16[2,4,128,2,128]{4,2,3,1,0:T(8,128)(2,1)}) %reduce-scatter.2.cloned.1.call-update) | async-done | bytes 524304 | tf_op jit(solution)/shard_map/reduce_scatter | solution.py:93
  282.4 2.6 copy.76
  (21 shorter events, 0.1 us)
Async XLA Ops:
  6.5 163.1 %all-gather.2.cloned.1.call-start = ((), (), s32[]{:S(2)}) async-start(), calls=%async_computation.2 | async-start | bytes 4718592 | tf_op jit(solution)/shard_map/all_gather | solution.py:60
  18.7 13.0 %copy-start.4 = (bf16[2,16,4]{1,2,0:T(4,128)(2,1)S(1)}, bf16[2,16,4]{1,2,0:T(4,128)(2,1)}, u32[]{:S(2)}) copy-start(bf16[2,16,4]{1,2,0:T(4,128)(2,1)} %param.7) | copy-start | bytes 772
  18.7 13.0 %copy-start.5 = (s32[4,4,128]{2,1,0:T(4,128)S(1)}, s32[4,4,128]{2,1,0:T(4,128)}, u32[]{:S(2)}) copy-start(s32[4,4,128]{2,1,0:T(4,128)} %param.11) | copy-start | bytes 24580
  18.7 148.7 %copy-start = (bf16[4,4,128,2,128]{4,3,2,1,0:T(2,128)(2,1)S(1)}, bf16[4,4,128,2,128]{4,3,2,1,0:T(2,128)(2,1)}, u32[]{:S(2)}) copy-start(bf16[4,4,128,2,128]{4,3,2,1,0:T(2,128)(2,1)} %param.8) | copy-start | bytes 3145732
  18.7 171.8 %all-to-all-start = ((bf16[4,4,128,4,2,128]{5,3,1,0,4,2:T(4,128)(2,1)}), bf16[4,4,128,4,2,128]{5,3,1,0,4,2:T(4,128)(2,1)}, u32[]{:S(2)}, u32[]{:S(2)}) async-start(bf16[4,4,128,4,2,128]{5,3,1,0,4,2:T(4,128)(2,1)} %copy.68), calls=%async_computation | async-start | bytes 8388608 | tf_op jit(solution)/shard_map/all_to_all | solution.py:55
  31.7 250.7 %reduce-scatter.2.cloned.1.call-start = ((), (), s32[]{:S(2)}) async-start(), calls=%async_computation.3 | async-start | bytes 4718592 | tf_op jit(solution)/shard_map/reduce_scatter | solution.py:93
  169.6 5.2 %copy-start.1 = (s32[4,128,128]{2,1,0:T(8,128)S(1)}, s32[4,128,128]{2,1,0:T(8,128)}, u32[]{:S(2)}) copy-start(s32[4,128,128]{2,1,0:T(8,128)} %param.9) | copy-start | bytes 786436
  169.6 5.1 %copy-start.6 = (s32[4]{0:T(128)S(1)}, s32[4]{0:T(128)}, u32[]{:S(2)}) copy-start(s32[4]{0:T(128)} %iota_add_fusion) | copy-start | bytes 52
  179.4 3.1 %copy-start.2 = (bf16[1,128,2,128]{3,1,0,2:T(8,128)(2,1)S(1)}, bf16[1,128,2,128]{3,1,0,2:T(8,128)(2,1)}, u32[]{:S(2)}) copy-start(bf16[1,128,2,128]{3,1,0,2:T(8,128)(2,1)} %get-tuple-element.15) | copy-start | bytes 196612
  179.4 3.1 %copy-start.3 = (bf16[1,128,2,128]{3,1,0,2:T(8,128)(2,1)S(1)}, bf16[1,128,2,128]{3,1,0,2:T(8,128)(2,1)}, u32[]{:S(2)}) copy-start(bf16[1,128,2,128]{3,1,0,2:T(8,128)(2,1)} %get-tuple-element.16) | copy-start | bytes 196612
Sparse Core Ops, SparseCore 0:
  9.1 79.6 all-gather.1
  234.8 47.5 reduce-scatter.1
where the time goes:
time: 292 us
  blocking collectives  135 us (46%)
  waiting for transfers between devices  47.8 us (16%)
  matrix products  35.8 us (12%)
  other arithmetic  26 us (9%)
  local copies, waits for them, and re-layouts  20.6 us (7%)
  between operations  13.6 us (5%)
  starting transfers between devices  13 us (4%)
    all_gather x1, blocking collectives, shards(): lax.all_gather(sample_mask.astype(jnp.bfloat16), 'space', axis=1, tiled=T...  135 us
    reduce_scatter x1, waiting for transfers between devices, shards(): lax.psum_scatter(jnp.einsum('txypz,tplq->lxyqz', combined, adjoint_mix(se...  47.7 us
    dot_general x3, matrix products, transform(): return jnp.einsum(form, volume, table, preferred_element_type=jnp.float32)  23 us
    all_to_all x1, starting transfers between devices, shards(): lax.all_to_all(data_first, 'space', split_axis=2, concat_axis=3, tiled=True)  12.9 us
    add x1, other arithmetic, shards(): combined_real = cosine * sum_real + sine * sum_imaginary  9.64 us
    dot_general x1, matrix products, shards(): jnp.einsum('txypz,tplq->lxyqz', combined, adjoint_mix(section), precision...  7.99 us
    convert_element_type x1, local copies, waits for them, and re-layouts, shards(): measured.astype(jnp.float32)  7.58 us
  transfers between devices with their start and end apart: 3, of which 1 were waited for; matrix products, arithmetic and copies ran while one was open for 12% of the time, Pallas kernels for 0%

commit v1 on v0

--- a/solution.py
+++ b/solution.py
@@ -53,7 +53,13 @@
         kspace_data, dft_table(kspace_data.shape[2], 1.0), "ctxypz,pxqk->ctkyqz"
     ).astype(jnp.bfloat16)
     measured = lax.all_to_all(data_first, "space", split_axis=2, concat_axis=3, tiled=True)
-    mask_all = lax.all_gather(sample_mask.astype(jnp.bfloat16), "space", axis=1, tiled=True)
+    attach_frame_by_axis = lambda field, device_axis: jnp.concatenate(
+        lax.all_to_all(
+            jnp.stack([field for _ in range(lax.axis_size(device_axis))]), device_axis, 0, 0
+        ),
+        axis=1,
+    )
+    mask_all = attach_frame_by_axis(sample_mask.astype(jnp.bfloat16), "space")
     mask_all = mask_all.astype(jnp.float32)[None, :, None, :, None, :]
     image = jnp.einsum(
         "lxypz,lptq->txyqz",

time: 292 us -> 255 us (0.87)
  blocking collectives: 135 us -> 0 us
  waiting for transfers between devices: 47.8 us -> 136 us
  starting transfers between devices: 13 us -> 21.6 us
    all_gather x1 -> x0, blocking collectives: 135 us -> none  [shards(): lax.all_gather(sample_mask.astype(jnp.bfloat16), 'space', axis=1, tiled=T...]
    all_to_all x1, waiting for transfers between devices: 0.01 us -> 35.9 us  [shards(): lax.all_to_all(data_first, 'space', split_axis=2, concat_axis=3, tiled=True)]
    all_gather x1, waiting for transfers between devices: 0.02 us -> 35.4 us  [shards(): lax.all_gather(spatial_coef, 'coil', axis=0, tiled=True)]
    reduce_scatter x1, waiting for transfers between devices: 47.7 us -> 63.4 us  [shards(): lax.psum_scatter(jnp.einsum('txypz,tplq->lxyqz', combined, adjoint_mix(se...]
    all_to_all x0 -> x1, starting transfers between devices: none -> 12.8 us  [shards(): lax.all_to_all(jnp.stack([field for _ in range(lax.axis_size(device_axis)...]
    all_to_all x1, starting transfers between devices: 12.9 us -> 8.82 us  [shards(): lax.all_to_all(data_first, 'space', split_axis=2, concat_axis=3, tiled=True)]
  transfers between devices with their start and end apart: 3 -> 4, of which waited for: 1 -> 4; matrix products, arithmetic and copies ran while one was open for 12% -> 14% of each run, Pallas kernels for 0% -> 0%
where the time goes in v1:
time: 255 us; the launch traced here: 254 us
  waiting for transfers between devices  136 us (53%)
  matrix products  36 us (14%)
  other arithmetic  26 us (10%)
  starting transfers between devices  21.6 us (8%)
  local copies, waits for them, and re-layouts  21.4 us (8%)
  between operations  13.6 us (5%)
    reduce_scatter x1, waiting for transfers between devices, shards(): lax.psum_scatter(jnp.einsum('txypz,tplq->lxyqz', combined, adjoint_mix(se...  63.4 us
    all_to_all x1, waiting for transfers between devices, shards(): lax.all_to_all(data_first, 'space', split_axis=2, concat_axis=3, tiled=True)  35.9 us
    all_gather x1, waiting for transfers between devices, shards(): lax.all_gather(spatial_coef, 'coil', axis=0, tiled=True)  35.4 us
    dot_general x3, matrix products, transform(): return jnp.einsum(form, volume, table, preferred_element_type=jnp.float32)  23.1 us
    all_to_all x1, starting transfers between devices, shards(): lax.all_to_all(jnp.stack([field for _ in range(lax.axis_size(device_axis)...  12.8 us
    add x1, other arithmetic, shards(): combined_real = cosine * sum_real + sine * sum_imaginary  9.64 us
    all_to_all x1, starting transfers between devices, shards(): lax.all_to_all(data_first, 'space', split_axis=2, concat_axis=3, tiled=True)  8.82 us
    dot_general x1, matrix products, shards(): jnp.einsum('txypz,tplq->lxyqz', combined, adjoint_mix(section), precision...  7.98 us
  transfers between devices with their start and end apart: 4, of which 4 were waited for; matrix products, arithmetic and copies ran while one was open for 14% of the time, Pallas kernels for 0%

profile of v1, /device:TPU:1, one launch (start us, length us, event | category | flops | bytes accessed | tf_op | source)
XLA Modules:
  0.0 254.3 jit_solution(9410371731216587550)
XLA Ops:
  6.5 0.0 all-gather.2.cloned.1.call-start
  6.5 1.9 copy.60
  8.5 0.0 all-gather.2.cloned.1.call-update
  8.5 0.7 convert_element_type.156
  9.2 0.7 stack.76
  9.9 12.8 %all-to-all-start = ((bf16[32,4,4,128]{3,2,1,0:T(4,128)(2,1)}), bf16[32,4,4,128]{3,2,1,0:T(4,128)(2,1)S(1)}, u32[]{:S(2)}, u32[]{:S(2)}) async-start(bf16[32,4,4,128]{3,2,1,0:T(4,128)(2,1)} %stack.76), calls=%async_computation | async-start | bytes 262144 | tf_op jit(solution)/shard_map/all_to_all | solution.py:57
  22.7 0.3 negate_convert_fusion
  22.9 0.3 multiply_convert_fusion
  23.2 0.3 multiply_convert_fusion.2
  23.5 3.7 %fusion.5 = bf16[4,4,128,4,2,128]{5,2,3,1,0,4:T(8,128)(2,1)S(1)} fusion(bf16[4,4,128,4,2,128]{5,4,3,2,1,0:T(2,128)(2,1)} %param.10, bf16[1,128,2,128]{3,1,2,0:T(8,128)(2,1)S(1)} %get-tuple-element.17, bf16[1,128,2,128]{3,1,2,0:T(8,128)(2,1)S(1)} %get-tuple-element.18), kind=kOutput, calls=%fused_computation.9 | convolution fusion | flops 1075904512 | bytes 8519680 | tf_op jit(solution)/shard_map/ctxypz,pxqk->ctkyqz/dot_general | solution.py:46
  27.2 5.2 %copy.66 = bf16[4,4,128,4,2,128]{5,3,1,0,4,2:T(4,128)(2,1)} copy(bf16[4,4,128,4,2,128]{5,2,3,1,0,4:T(8,128)(2,1)S(1)} %fusion.5) | data formatting | bytes 8388608 | tf_op jit(solution)/shard_map/convert_element_type | solution.py:54
  32.4 1.2 all-to-all-done
  33.6 8.8 %all-to-all-start.1 = ((bf16[4,4,128,4,2,128]{5,3,1,0,4,2:T(4,128)(2,1)}), bf16[4,4,128,4,2,128]{5,3,1,0,4,2:T(4,128)(2,1)}, u32[]{:S(2)}, u32[]{:S(2)}) async-start(bf16[4,4,128,4,2,128]{5,3,1,0,4,2:T(4,128)(2,1)} %copy.66), calls=%async_computation.1 | async-start | bytes 8388608 | tf_op jit(solution)/shard_map/all_to_all | solution.py:55
  42.4 0.0 reduce-scatter.2.cloned.1.call-start
  42.5 0.5 iota_add_fusion
  43.0 2.2 slice_convert_fusion.1
  45.3 35.4 %all-gather.2.cloned.1.call-done = bf16[16,4,128,2,128]{4,2,3,1,0:T(8,128)(2,1)} async-done(((bf16[2,4,128,2,128]{4,2,3,1,0:T(8,128)(2,1)}), bf16[16,4,128,2,128]{4,2,3,1,0:T(8,128)(2,1)}) %all-gather.2.cloned.1.call-update) | async-done | bytes 4194320 | tf_op jit(solution)/shard_map/all_gather | solution.py:66
  80.7 4.9 %fusion.36 = f32[4,2,4,128,128]{4,0,3,2,1:T(4,128)S(1)} fusion(bf16[16,4,128,2,128]{4,2,3,1,0:T(8,128)(2,1)} %all-gather.2.cloned.1.call-done, bf16[16,1,4,2]{0,2,1,3:T(4,128)(2,1)S(1)} %get-tuple-element.26, bf16[16,1,4,2]{0,2,1,3:T(4,128)(2,1)S(1)} %get-tuple-element.25), kind=kOutput, calls=%fused_computation.43 | convolution fusion | flops 33555456 | bytes 6291968 | tf_op jit(solution)/shard_map/lxypz,lptq->txyqz/dot_general | solution.py:64
  85.6 0.3 copy.120
  85.9 4.6 %multiply_subtract_fusion = (f32[4,4,128,128]{3,2,1,0:T(8,128)S(1)}, f32[4,4,128,128]{3,2,1,0:T(8,128)S(1)}) fusion(f32[4,4,128,2,128]{4,2,1,0,3:T(8,128)S(1)} %bitcast.239, s32[4]{0:T(128)S(1)} %copy-done.3, s32[4,128,128]{2,1,0:T(8,128)S(1)} %copy-done.1), kind=kLoop, calls=%fused_computation.64 | loop fusion | flops 5242880 | bytes 4456464 | tf_op jit(solution)/shard_map/sub | solution.py:73
  90.5 3.1 %subtract_convert_fusion = (bf16[4,4,4,128,1,128]{5,3,4,2,1,0:T(8,128)(2,1)}, bf16[4,4,4,128,1,128]{5,3,4,2,1,0:T(8,128)(2,1)}) fusion(f32[4,4,128,128]{3,2,1,0:T(8,128)S(1)} %get-tuple-element.12, f32[4,4,128,128]{3,2,1,0:T(8,128)S(1)} %bitcast.237, f32[4,4,128,128]{3,2,1,0:T(8,128)S(1)} %get-tuple-element.11, f32[4,4,128,128]{3,2,1,0:T(8,128)S(1)} %bitcast.235), kind=kLoop, calls=%fused_computation.30 | loop fusion | flops 8388608 | bytes 8388608 | tf_op jit(solution)/shard_map/convert.7
  93.6 8.0 %fusion.3 = f32[2,128,4,4,4,128,1]{5,1,6,0,4,3,2:T(8,128)} fusion(bf16[4,4,4,128,1,128]{5,3,4,2,1,0:T(8,128)(2,1)} %get-tuple-element.8, bf16[4,4,4,128,1,128]{5,3,4,2,1,0:T(8,128)(2,1)} %get-tuple-element.7, bf16[1,128,2,128]{3,1,0,2:T(8,128)(2,1)S(1)} %get-tuple-element.16, bf16[1,128,2,128]{3,1,0,2:T(8,128)(2,1)S(1)} %get-tuple-element.15), kind=kOutput, calls=%fused_computation.8 | convolution fusion | flops 2158493696 | bytes 12713984 | tf_op jit(solution)/shard_map/ctxypz,pyqk->ctxkqz/dot_general | solution.py:46
  101.5 35.9 %all-to-all-done.1 = bf16[4,4,128,4,2,128]{5,3,1,0,4,2:T(4,128)(2,1)} async-done(((bf16[4,4,128,4,2,128]{5,3,1,0,4,2:T(4,128)(2,1)}), bf16[4,4,128,4,2,128]{5,3,1,0,4,2:T(4,128)(2,1)}, u32[]{:S(2)}, u32[]{:S(2)}) %all-to-all-start.1) | async-done | bytes 4194336 | tf_op jit(solution)/shard_map/all_to_all | solution.py:55
  137.4 7.6 %copy.67 = f32[4,4,32,4,4,2,128]{6,4,2,5,3,1,0:T(4,128)} copy(bf16[4,4,32,4,4,2,128]{6,4,1,0,5,3,2:T(4,128)(2,1)} %bitcast.90) | data formatting | bytes 12582912 | tf_op jit(solution)/shard_map/convert_element_type | solution.py:86
  145.0 11.5 %fusion.27 = f32[4,4,4,128,2,128]{5,3,4,2,1,0:T(8,128)} fusion(f32[4,4,4,128,2,128]{5,3,4,2,1,0:T(8,128)} %bitcast.234, f32[2,128,4,4,4,128,1]{5,1,6,0,4,3,2:T(8,128)} %fusion.3, f32[4,128,128]{2,1,0:T(8,128)S(1)} %bitcast.240, bf16[1,128,2,128]{3,1,2,0:T(8,128)(2,1)S(1)} %get-tuple-element.17, bf16[1,128,2,128]{3,1,2,0:T(8,128)(2,1)S(1)} %get-tuple-element.18), kind=kOutput, calls=%fused_computation.32 | convolution fusion | flops 2156396544 | bytes 25559040 | tf_op jit(solution)/shard_map/ctxypz,pzqk->ctxyqk/dot_general | solution.py:46
  156.5 4.3 %add_reduce_fusion = (f32[4,4,128,128]{3,2,1,0:T(8,128)S(1)}, f32[4,4,128,128]{3,2,1,0:T(8,128)S(1)}) fusion(f32[4,4,4,128,2,128]{5,3,4,2,1,0:T(8,128)} %fusion.27, f32[4,4,128,128]{3,2,1,0:T(8,128)S(1)} %bitcast.238, f32[4,4,128,128]{3,2,1,0:T(8,128)S(1)} %bitcast.236), kind=kLoop, calls=%fused_computation.28 | loop fusion | flops 7864320 | bytes 12582912 | tf_op jit(solution)/shard_map/reduce_sum | solution.py:93
  160.8 9.6 %fusion.45 = (f32[4,4,128,1,128]{4,0,3,2,1:T(4,128)S(1)}, f32[4,4,128,1,128]{4,0,3,2,1:T(4,128)S(1)}) fusion(f32[4,4,128,128]{3,2,1,0:T(8,128)S(1)} %get-tuple-element.6, f32[4,4,128,128]{3,2,1,0:T(8,128)S(1)} %get-tuple-element.5, s32[4]{0:T(128)S(1)} %copy-done.3, s32[4,128,128]{2,1,0:T(8,128)S(1)} %copy-done.1), kind=kLoop, calls=%fused_computation.58 | loop fusion | flops 5242880 | bytes 4456464 | tf_op jit(solution)/shard_map/add | solution.py:95
  170.5 8.0 %fusion.6 = bf16[16,4,128,2,128]{4,0,2,1,3:T(8,128)(2,1)S(1)} fusion(f32[4,4,128,1,128]{4,0,3,2,1:T(4,128)S(1)} %get-tuple-element.10, f32[4,4,128,1,128]{4,0,3,2,1:T(4,128)S(1)} %get-tuple-element.9, f32[4,1,16,2]{2,0,1,3:T(4,128)S(1)} %get-tuple-element.22, f32[4,1,16,2]{2,0,1,3:T(4,128)S(1)} %get-tuple-element.21), kind=kOutput, calls=%fused_computation.10 | convolution fusion | flops 203948288 | bytes 6292480 | tf_op jit(solution)/shard_map/txypz,tplq->lxyqz/dot_general | solution.py:100
  178.5 3.1 %copy.73 = bf16[16,4,128,2,128]{4,2,3,1,0:T(8,128)(2,1)} copy(bf16[16,4,128,2,128]{4,0,2,1,3:T(8,128)(2,1)S(1)} %fusion.6) | data formatting | bytes 8388608 | tf_op jit(solution)/shard_map/convert_element_type | solution.py:102
  181.5 0.0 reduce-scatter.2.cloned.1.call-update
  181.6 63.4 %reduce-scatter.2.cloned.1.call-done = bf16[2,4,128,2,128]{4,2,3,1,0:T(8,128)(2,1)} async-done(((bf16[16,4,128,2,128]{4,2,3,1,0:T(8,128)(2,1)}), bf16[2,4,128,2,128]{4,2,3,1,0:T(8,128)(2,1)}) %reduce-scatter.2.cloned.1.call-update) | async-done | bytes 524304 | tf_op jit(solution)/shard_map/reduce_scatter | solution.py:99
  245.0 2.6 %copy.74 = f32[2,4,128,2,128]{4,3,2,1,0:T(2,128)} copy(bf16[2,4,128,2,128]{4,2,3,1,0:T(8,128)(2,1)} %reduce-scatter.2.cloned.1.call-done) | data formatting | bytes 1572864 | tf_op jit(solution)/shard_map/convert_element_type | solution.py:106
  (18 shorter events, 0.1 us)
Async XLA Ops:
  6.5 74.2 %all-gather.2.cloned.1.call-start = ((), (), s32[]{:S(2)}) async-start(), calls=%async_computation.3 | async-start | bytes 4718592 | tf_op jit(solution)/shard_map/all_gather | solution.py:66
  9.9 23.7 %all-to-all-start = ((bf16[32,4,4,128]{3,2,1,0:T(4,128)(2,1)}), bf16[32,4,4,128]{3,2,1,0:T(4,128)(2,1)S(1)}, u32[]{:S(2)}, u32[]{:S(2)}) async-start(bf16[32,4,4,128]{3,2,1,0:T(4,128)(2,1)} %stack.76), calls=%async_computation | async-start | bytes 262144 | tf_op jit(solution)/shard_map/all_to_all | solution.py:57
  32.4 10.1 %copy-start.2 = (bf16[2,16,4]{1,2,0:T(4,128)(2,1)S(1)}, bf16[2,16,4]{1,2,0:T(4,128)(2,1)}, u32[]{:S(2)}) copy-start(bf16[2,16,4]{1,2,0:T(4,128)(2,1)} %param.7) | copy-start | bytes 772
  32.4 10.6 %copy-start = (bf16[4,4,128,2,128]{4,3,2,1,0:T(2,128)(2,1)S(1)}, bf16[4,4,128,2,128]{4,3,2,1,0:T(2,128)(2,1)}, u32[]{:S(2)}) copy-start(bf16[4,4,128,2,128]{4,3,2,1,0:T(2,128)(2,1)} %param.8) | copy-start | bytes 3145732
  33.6 103.8 %all-to-all-start.1 = ((bf16[4,4,128,4,2,128]{5,3,1,0,4,2:T(4,128)(2,1)}), bf16[4,4,128,4,2,128]{5,3,1,0,4,2:T(4,128)(2,1)}, u32[]{:S(2)}, u32[]{:S(2)}) async-start(bf16[4,4,128,4,2,128]{5,3,1,0,4,2:T(4,128)(2,1)} %copy.66), calls=%async_computation.1 | async-start | bytes 8388608 | tf_op jit(solution)/shard_map/all_to_all | solution.py:55
  42.4 202.5 %reduce-scatter.2.cloned.1.call-start = ((), (), s32[]{:S(2)}) async-start(), calls=%async_computation.4 | async-start | bytes 4718592 | tf_op jit(solution)/shard_map/reduce_scatter | solution.py:99
  80.7 5.1 %copy-start.1 = (s32[4,128,128]{2,1,0:T(8,128)S(1)}, s32[4,128,128]{2,1,0:T(8,128)}, u32[]{:S(2)}) copy-start(s32[4,128,128]{2,1,0:T(8,128)} %param.9) | copy-start | bytes 786436
  80.7 5.1 %copy-start.3 = (s32[4]{0:T(128)S(1)}, s32[4]{0:T(128)}, u32[]{:S(2)}) copy-start(s32[4]{0:T(128)} %iota_add_fusion) | copy-start | bytes 52
Sparse Core Ops, SparseCore 0:
  9.1 71.5 all-gather.1
  181.7 63.2 reduce-scatter.1
